TPU v7x, 128 devices: a whole 4x4x4 slice. The times are simulated.
128 devices in a mesh: seq: 8 (over z, core), blk: 4 (over y), tp: 4 (over x).
Axes of the slice: x: 4, y: 4, z: 4, core: 2. Of those that a mesh axis runs over, the one named last changes fastest.
Arguments:
- hidden_in: bfloat16 [16384, 1024], P(('seq', 'blk', 'tp')), may hold values from -24 to 24
- ln1_gain: float32 [1024], replicated, may hold values from 0.1 to 1.9
- ln1_bias: float32 [1024], replicated, may hold values from -3 to 3
- qkv_weight: bfloat16 [1024, 3072], replicated, may hold values from -0.1875 to 0.1875
- qv_bias: float32 [2, 1024], replicated, may hold values from -3 to 3
- out_weight: bfloat16 [1024, 1024], replicated, may hold values from -0.75 to 0.75
- out_bias: float32 [1024], replicated, may hold values from -3 to 3
- ln2_gain: float32 [1024], replicated, may hold values from 0.1 to 1.9
- ln2_bias: float32 [1024], replicated, may hold values from -3 to 3
- fc_weight: bfloat16 [1024, 4096], P(None, 'tp'), may hold values from -0.1875 to 0.1875
- fc_bias: float32 [4096], P('tp'), may hold values from -3 to 3
- proj_weight: bfloat16 [4096, 1024], P('tp'), may hold values from -0.09375 to 0.09375
- proj_bias: float32 [1024], replicated, may hold values from -3 to 3
- cotangent: float32 [16384, 1024], P(('seq', 'blk', 'tp')), may hold values from -3 to 3
Outputs:
- block_out: float32 [16384, 1024], P(('seq', 'blk', 'tp'))
- input_grad: float32 [16384, 1024], P(('seq', 'blk', 'tp'))
- ln1_gain_grad: float32 [1024], P(('seq', 'blk'))
- ln1_bias_grad: float32 [1024], P(('seq', 'blk'))
- qkv_weight_grad: float32 [1024, 3072], P(('seq', 'blk'))
- qv_bias_grad: float32 [2, 1024], P(None, ('seq', 'blk'))
- out_weight_grad: float32 [1024, 1024], P(('seq', 'blk'))
- out_bias_grad: float32 [1024], P(('seq', 'blk'))
- ln2_gain_grad: float32 [1024], P(('seq', 'blk'))
- ln2_bias_grad: float32 [1024], P(('seq', 'blk'))
- fc_weight_grad: float32 [1024, 4096], P(None, 'tp')
- fc_bias_grad: float32 [4096], P('tp')
- proj_weight_grad: float32 [4096, 1024], P('tp')
- proj_bias_grad: float32 [1024], P(('seq', 'blk'))
All inputs are finite; a program needn't handle non-finite values.
Results may differ from a plain program's by a relative error of at most 0.025.
Values may be sent and summed in bfloat16 or wider, within the bound.
A program may use at most 128 MiB of HBM per device.

v0:
```python
import math
import jax
import jax.numpy as jnp
from jax import lax
from jax.sharding import PartitionSpec as P

HEADS = 16
HEAD_DIM = 64
epsilon = 1e-05
gelu_coef = math.sqrt(2.0 / math.pi)
masked_score = -1e30


def normalize(matrix, norm_gain, norm_shift):
    row_mean = jnp.mean(matrix, axis=-1, keepdims=True)
    centered = matrix - row_mean
    variance = jnp.mean(centered * centered, axis=-1, keepdims=True)
    inverse = lax.rsqrt(variance + epsilon)
    scaled = centered * inverse
    return (scaled, inverse, scaled * norm_gain + norm_shift)


def norm_back(upstream_grad, scaled, inverse, norm_gain):
    weighted = upstream_grad * norm_gain
    first_mean = jnp.mean(weighted, axis=-1, keepdims=True)
    second_mean = jnp.mean(weighted * scaled, axis=-1, keepdims=True)
    return inverse * (weighted - first_mean - scaled * second_mean)


def gelu_pair(hidden_pre):
    tanh_arg = gelu_coef * (hidden_pre + 0.044715 * hidden_pre * hidden_pre * hidden_pre)
    tanh_value = jnp.tanh(tanh_arg)
    gelu_value = 0.5 * hidden_pre * (1.0 + tanh_value)
    gelu_slope = 0.5 * (1.0 + tanh_value) + 0.5 * hidden_pre * (
        1.0 - tanh_value * tanh_value
    ) * gelu_coef * (1.0 + 3.0 * 0.044715 * hidden_pre * hidden_pre)
    return (gelu_value, gelu_slope)


def per_device(
    hidden_in,
    ln1_gain,
    ln1_bias,
    qkv_weight,
    qv_bias,
    out_weight,
    out_bias,
    ln2_gain,
    ln2_bias,
    fc_weight,
    fc_bias,
    proj_weight,
    proj_bias,
    cotangent,
):
    local_tokens, model_width = hidden_in.shape
    seq_count = lax.axis_size("seq")
    cycle_size = lax.axis_size(("blk", "tp"))
    local_heads = HEADS // seq_count
    head_dim = HEAD_DIM
    query_rows = seq_count * local_tokens
    head_cols = model_width // seq_count
    score_scale = 1.0 / math.sqrt(head_dim)
    hidden_f = hidden_in.astype(jnp.float32)
    scaled_one, inverse_one, normed_one = normalize(hidden_f, ln1_gain, ln1_bias)
    normed_bf = normed_one.astype(jnp.bfloat16)
    weight_three = qkv_weight.reshape(model_width, 3, model_width)
    bias_three = jnp.stack([qv_bias[0], jnp.zeros_like(qv_bias[0]), qv_bias[1]])
    projected = jnp.einsum(
        "td,dcf->ctf", normed_bf, weight_three, preferred_element_type=jnp.float32
    )
    qkv_tokens = (projected + bias_three[:, None, :]).astype(jnp.bfloat16)
    qkv_heads = lax.all_to_all(qkv_tokens, "seq", split_axis=2, concat_axis=1, tiled=True)
    query_heads = qkv_heads[0]
    key_heads = qkv_heads[1]
    value_heads = qkv_heads[2]
    cycle_index = lax.axis_index(("blk", "tp"))
    local_index = jnp.arange(query_rows, dtype=jnp.int32)
    query_place = (
        local_index // local_tokens * cycle_size + cycle_index
    ) * local_tokens + local_index % local_tokens

    def key_positions(first_key, key_count):
        gathered = first_key + jnp.arange(key_count, dtype=jnp.int32)
        within = gathered % query_rows
        return (
            within // local_tokens * cycle_size + gathered // query_rows
        ) * local_tokens + within % local_tokens

    def split_heads(matrix):
        return matrix.reshape(matrix.shape[0], local_heads, head_dim)

    def block_scores(low_row, key_block):
        return (
            jnp.einsum(
                "qhd,khd->hqk",
                split_heads(query_heads[low_row:]),
                split_heads(key_block),
                preferred_element_type=jnp.float32,
            )
            * score_scale
        )

    def visible_of(low_row, key_block, first_key):
        return (
            query_place[low_row:, None] >= key_positions(first_key, key_block.shape[0])[None, :]
        )[None]

    def forward_update(softmax_state, key_block, value_block, first_key, low_row):
        run_max, run_sum, run_acc = softmax_state
        visible = visible_of(low_row, key_block, first_key)
        scores = jnp.where(visible, block_scores(low_row, key_block), masked_score)
        old_max = run_max[:, low_row:]
        new_max = jnp.maximum(old_max, jnp.max(scores, axis=2))
        rescale = jnp.exp(old_max - new_max)
        attn_prob = jnp.where(visible, jnp.exp(scores - new_max[:, :, None]), 0.0)
        new_sum = run_sum[:, low_row:] * rescale + jnp.sum(attn_prob, axis=2)
        weighted_values = jnp.einsum(
            "hqk,khd->qhd",
            attn_prob.astype(jnp.bfloat16),
            split_heads(value_block),
            preferred_element_type=jnp.float32,
        ).reshape(query_rows - low_row, head_cols)
        new_acc = run_acc[low_row:] * jnp.repeat(rescale.T, head_dim, axis=1) + weighted_values
        return (
            run_max.at[:, low_row:].set(new_max),
            run_sum.at[:, low_row:].set(new_sum),
            run_acc.at[low_row:].set(new_acc),
        )

    def by_segments(update, carry_state, key_shard, value_shard, first_key):
        for segment in range(seq_count):
            low_row = segment * local_tokens
            carry_state = update(
                carry_state,
                key_shard[low_row : low_row + local_tokens],
                value_shard[low_row : low_row + local_tokens],
                first_key + low_row,
                low_row,
            )
        return carry_state

    def fold_with(update, carry_state, shard_pair):
        key_piece, value_piece = shard_pair
        piece_rows = key_piece.shape[0]

        def shard_step(shard_number, inner_state):
            offset = shard_number * query_rows
            key_shard = lax.dynamic_slice_in_dim(key_piece, offset, query_rows, 0)
            value_shard = lax.dynamic_slice_in_dim(value_piece, offset, query_rows, 0)
            return by_segments(update, inner_state, key_shard, value_shard, offset)

        return lax.fori_loop(0, piece_rows // query_rows, shard_step, carry_state)

    initial_state = (
        jnp.full((local_heads, query_rows), masked_score, jnp.float32),
        jnp.zeros((local_heads, query_rows), jnp.float32),
        jnp.zeros((query_rows, head_cols), jnp.float32),
    )
    cycle_init = (initial_state,)
    run_max, run_sum, run_acc = fold_with(
        forward_update,
        cycle_init[0],
        (
            lax.all_gather(key_heads, ("blk", "tp"), axis=0, tiled=True),
            lax.all_gather(value_heads, ("blk", "tp"), axis=0, tiled=True),
        ),
    )
    context_heads = (run_acc / jnp.repeat(run_sum.T, head_dim, axis=1)).astype(jnp.bfloat16)
    log_total = run_max + jnp.log(run_sum)
    context_tokens = lax.all_to_all(context_heads, "seq", split_axis=0, concat_axis=1, tiled=True)
    residual = (
        hidden_f
        + jnp.dot(context_tokens, out_weight, preferred_element_type=jnp.float32)
        + out_bias
    )
    scaled_two, inverse_two, normed_two = normalize(residual, ln2_gain, ln2_bias)
    normed_two_bf = normed_two.astype(jnp.bfloat16)
    gathered_norm = lax.all_gather(normed_two_bf, "tp", axis=0, tiled=True)
    hidden_pre = jnp.dot(gathered_norm, fc_weight, preferred_element_type=jnp.float32) + fc_bias
    gelu_value, gelu_slope = gelu_pair(hidden_pre)
    activation = gelu_value.astype(jnp.bfloat16)
    mlp_out = lax.psum_scatter(
        jnp.dot(activation, proj_weight, preferred_element_type=jnp.float32).astype(jnp.bfloat16),
        "tp",
        scatter_dimension=0,
        tiled=True,
    ).astype(jnp.float32)
    block_out = residual + mlp_out + proj_bias
    cot_bf = cotangent.astype(jnp.bfloat16)
    gathered_cot = lax.all_gather(cot_bf, "tp", axis=0, tiled=True)
    hidden_grad = (
        jnp.dot(gathered_cot, proj_weight.T, preferred_element_type=jnp.float32) * gelu_slope
    )
    hidden_grad_bf = hidden_grad.astype(jnp.bfloat16)
    proj_weight_grad = jnp.einsum(
        "tf,td->fd", activation, gathered_cot, preferred_element_type=jnp.float32
    )
    fc_weight_grad = jnp.einsum(
        "td,tf->df", gathered_norm, hidden_grad_bf, preferred_element_type=jnp.float32
    )
    fc_bias_grad = jnp.sum(hidden_grad, axis=0)
    normed_two_grad = lax.psum_scatter(
        jnp.dot(hidden_grad_bf, fc_weight.T, preferred_element_type=jnp.float32).astype(
            jnp.bfloat16
        ),
        "tp",
        scatter_dimension=0,
        tiled=True,
    ).astype(jnp.float32)
    residual_grad = cotangent + norm_back(normed_two_grad, scaled_two, inverse_two, ln2_gain)
    residual_grad_bf = residual_grad.astype(jnp.bfloat16)
    context_grad = jnp.dot(
        residual_grad_bf, out_weight.T, preferred_element_type=jnp.float32
    ).astype(jnp.bfloat16)
    context_grad_heads = lax.all_to_all(
        context_grad, "seq", split_axis=1, concat_axis=0, tiled=True
    )
    delta_rows = jnp.sum(
        split_heads(context_grad_heads).astype(jnp.float32)
        * split_heads(context_heads).astype(jnp.float32),
        axis=2,
    ).T

    def backward_update(grad_state, key_block, value_block, first_key, low_row):
        query_grad, key_grad, value_grad = grad_state
        visible = visible_of(low_row, key_block, first_key)
        attn_prob = jnp.where(
            visible, jnp.exp(block_scores(low_row, key_block) - log_total[:, low_row:, None]), 0.0
        )
        grad_rows = split_heads(context_grad_heads[low_row:])
        prob_grad = jnp.einsum(
            "qhd,khd->hqk", grad_rows, split_heads(value_block), preferred_element_type=jnp.float32
        )
        score_grad = (attn_prob * (prob_grad - delta_rows[:, low_row:, None]) * score_scale).astype(
            jnp.bfloat16
        )
        query_part = jnp.einsum(
            "hqk,khd->qhd", score_grad, split_heads(key_block), preferred_element_type=jnp.float32
        ).reshape(query_rows - low_row, head_cols)
        key_part = jnp.einsum(
            "hqk,qhd->khd",
            score_grad,
            split_heads(query_heads[low_row:]),
            preferred_element_type=jnp.float32,
        ).reshape(key_block.shape[0], head_cols)
        value_part = jnp.einsum(
            "hqk,qhd->khd",
            attn_prob.astype(jnp.bfloat16),
            grad_rows,
            preferred_element_type=jnp.float32,
        ).reshape(key_block.shape[0], head_cols)
        return (
            query_grad.at[low_row:].add(query_part),
            lax.dynamic_update_slice_in_dim(key_grad, key_part, first_key, 0),
            lax.dynamic_update_slice_in_dim(value_grad, value_part, first_key, 0),
        )

    grad_init = (
        jnp.zeros((query_rows, head_cols), jnp.float32),
        jnp.zeros((cycle_size * query_rows, head_cols), jnp.float32),
        jnp.zeros((cycle_size * query_rows, head_cols), jnp.float32),
    )
    query_grad, key_grad, value_grad = fold_with(
        backward_update,
        grad_init,
        (
            lax.all_gather(key_heads, ("blk", "tp"), axis=0, tiled=True),
            lax.all_gather(value_heads, ("blk", "tp"), axis=0, tiled=True),
        ),
    )
    key_own, value_own = (
        lax.psum_scatter(
            key_grad.astype(jnp.bfloat16), ("blk", "tp"), scatter_dimension=0, tiled=True
        ).astype(jnp.float32),
        lax.psum_scatter(
            value_grad.astype(jnp.bfloat16), ("blk", "tp"), scatter_dimension=0, tiled=True
        ).astype(jnp.float32),
    )
    head_grads = jnp.stack([query_grad, key_own, value_own]).astype(jnp.bfloat16)
    token_grads = lax.all_to_all(head_grads, "seq", split_axis=1, concat_axis=2, tiled=True)
    query_bias_grad = jnp.sum(token_grads[0].astype(jnp.float32), axis=0)
    value_bias_grad = jnp.sum(token_grads[2].astype(jnp.float32), axis=0)
    normed_one_grad = jnp.einsum(
        "ctf,dcf->td", token_grads, weight_three, preferred_element_type=jnp.float32
    )
    input_grad = residual_grad + norm_back(normed_one_grad, scaled_one, inverse_one, ln1_gain)
    vectors = jnp.stack(
        [
            jnp.sum(normed_one_grad * scaled_one, axis=0),
            jnp.sum(normed_one_grad, axis=0),
            query_bias_grad,
            value_bias_grad,
            jnp.sum(residual_grad, axis=0),
            jnp.sum(normed_two_grad * scaled_two, axis=0),
            jnp.sum(normed_two_grad, axis=0),
            jnp.sum(cotangent, axis=0),
        ],
        axis=1,
    )
    qkv_weight_grad = jnp.einsum(
        "td,ctf->dcf", normed_bf, token_grads, preferred_element_type=jnp.float32
    ).reshape(model_width, 3 * model_width)
    out_weight_grad = jnp.einsum(
        "tc,td->cd", context_tokens, residual_grad_bf, preferred_element_type=jnp.float32
    )
    qkv_part, out_part, vector_part = (
        lax.psum_scatter(
            qkv_weight_grad.astype(jnp.bfloat16), ("seq", "blk"), scatter_dimension=0, tiled=True
        ).astype(jnp.float32),
        lax.psum_scatter(
            out_weight_grad.astype(jnp.bfloat16), ("seq", "blk"), scatter_dimension=0, tiled=True
        ).astype(jnp.float32),
        lax.psum_scatter(
            vectors.astype(jnp.bfloat16), ("seq", "blk"), scatter_dimension=0, tiled=True
        ).astype(jnp.float32),
    )
    qkv_part, out_part, vector_part = (
        lax.psum(qkv_part.astype(jnp.bfloat16), "tp").astype(jnp.float32),
        lax.psum(out_part.astype(jnp.bfloat16), "tp").astype(jnp.float32),
        lax.psum(vector_part.astype(jnp.bfloat16), "tp").astype(jnp.float32),
    )
    fc_weight_grad, fc_bias_grad, proj_weight_grad = (
        lax.psum(fc_weight_grad.astype(jnp.bfloat16), ("seq", "blk")).astype(jnp.float32),
        lax.psum(fc_bias_grad.astype(jnp.bfloat16), ("seq", "blk")).astype(jnp.float32),
        lax.psum(proj_weight_grad.astype(jnp.bfloat16), ("seq", "blk")).astype(jnp.float32),
    )
    qv_bias_grad = jnp.stack([vector_part[:, 2], vector_part[:, 3]])
    return (
        block_out,
        input_grad,
        vector_part[:, 0],
        vector_part[:, 1],
        qkv_part,
        qv_bias_grad,
        out_part,
        vector_part[:, 4],
        vector_part[:, 5],
        vector_part[:, 6],
        fc_weight_grad,
        fc_bias_grad,
        proj_weight_grad,
        vector_part[:, 7],
    )


def solution(mesh):
    return jax.shard_map(
        per_device,
        mesh=mesh,
        in_specs=(
            P(("seq", "blk", "tp"), None),
            P(),
            P(),
            P(),
            P(),
            P(),
            P(),
            P(),
            P(),
            P(None, "tp"),
            P("tp"),
            P("tp", None),
            P(),
            P(("seq", "blk", "tp"), None),
        ),
        out_specs=(
            P(("seq", "blk", "tp"), None),
            P(("seq", "blk", "tp"), None),
            P(("seq", "blk")),
            P(("seq", "blk")),
            P(("seq", "blk"), None),
            P(None, ("seq", "blk")),
            P(("seq", "blk"), None),
            P(("seq", "blk")),
            P(("seq", "blk")),
            P(("seq", "blk")),
            P(None, "tp"),
            P("tp"),
            P("tp", None),
            P(("seq", "blk")),
        ),
        check_vma=False,
    )
```

profile of v0, /device:TPU:0, one launch (start us, length us, event | category | flops | bytes accessed | tf_op | source)
XLA Modules:
  0.0 1488.0 jit_solution(16899424603222186177)
XLA Ops:
  10.5 8.7 copy.287
  19.4 5.9 fusion.199
  27.6 21.5 %all_to_all.71 = bf16[3,128,1024]{1,0,2:T(4,128)(2,1)S(1)} all-to-all(bf16[3,128,1024]{1,0,2:T(4,128)(2,1)} %copy.289), channel_id=1, replica_groups=mesh['seq'=8,'blk'=4,'tp'=4] {'seq'}, dimensions={2} | all-to-all | bytes 1572864 | tf_op jit(solution)/shard_map/all_to_all | solution.py:73
  57.5 45.0 %all-gather.7.cloned.1.call-done = bf16[16384,128]{0,1:T(8,128)(2,1)} async-done(((bf16[1024,128]{0,1:T(8,128)(2,1)}), bf16[16384,128]{0,1:T(8,128)(2,1)}) %all-gather.7.cloned.1.call-update) | async-done | bytes 4194320 | tf_op jit(solution)/shard_map/all_gather | solution.py:166
  102.5 53.9 %all-gather.5.cloned.1.call-done = bf16[16384,128]{0,1:T(8,128)(2,1)} async-done(((bf16[1024,128]{0,1:T(8,128)(2,1)}), bf16[16384,128]{0,1:T(8,128)(2,1)}) %all-gather.5.cloned.1.call-update) | async-done | bytes 4194320 | tf_op jit(solution)/shard_map/all_gather | solution.py:165
  156.5 220.2 %while.112 = (s32[]{:T(128)}, f32[2,1024]{1,0:T(2,128)S(1)}, f32[2,1024]{1,0:T(2,128)S(1)}, f32[1024,128]{0,1:T(8,128)S(1)}, s32[1024]{0:T(1024)S(1)}, /*index=5...) while((s32[]{:T(128)}, f32[2,1024]{1,0:T(2,128)S(1)}, ...), condition=%wide.region_26.27_spmd, body=%wide.region_9.26_spmd.sunk | while | flops 314464256 | bytes 33136192 | solution.py:153
  378.6 11.8 all_to_all.72
  396.8 19.6 %all-gather.9.cloned.1.call-done = bf16[512,1024]{1,0:T(8,128)(2,1)} async-done(((bf16[128,1024]{1,0:T(8,128)(2,1)}), bf16[512,1024]{1,0:T(8,128)(2,1)}) %all-gather.9.cloned.1.call-update) | async-done | bytes 1048592 | tf_op jit(solution)/shard_map/all_gather | solution.py:179
  416.4 4.6 fusion.274
  420.9 21.8 %all-gather.11.cloned.1.call-done = bf16[512,1024]{1,0:T(8,128)(2,1)} async-done(((bf16[128,1024]{1,0:T(8,128)(2,1)}), bf16[512,1024]{1,0:T(8,128)(2,1)}) %all-gather.11.cloned.1.call-update) | async-done | bytes 1048592 | tf_op jit(solution)/shard_map/all_gather | solution.py:191
  442.8 4.4 fusion.257
  454.7 19.8 %reduce-scatter.12.cloned.1.call-done = bf16[128,1024]{1,0:T(8,128)(2,1)} async-done(((bf16[512,1024]{1,0:T(8,128)(2,1)}), bf16[128,1024]{1,0:T(8,128)(2,1)}) %reduce-scatter.12.cloned.1.call-update) | async-done | bytes 262160 | tf_op jit(solution)/shard_map/reduce_scatter | solution.py:203
  475.8 25.0 %reduce-scatter.10.cloned.1.call-done = bf16[128,1024]{1,0:T(8,128)(2,1)} async-done(((bf16[512,1024]{1,0:T(8,128)(2,1)}), bf16[128,1024]{1,0:T(8,128)(2,1)}) %reduce-scatter.10.cloned.1.call-update) | async-done | bytes 262160 | tf_op jit(solution)/shard_map/reduce_scatter | solution.py:183
  505.5 4.4 all-to-all-start.2
  510.1 7.3 all-to-all-done.2
  523.1 378.5 %while.113 = (s32[]{:T(128)}, f32[1024,128]{0,1:T(8,128)S(1)}, bf16[16384,128]{0,1:T(8,128)(2,1)}, bf16[16384,128]{0,1:T(8,128)(2,1)}, bf16[16384,128]{0,1:T(8,1...) while((s32[]{:T(128)}, f32[1024,128]{0,1:T(8,128)S(1)}, ...), condition=%wide.region_35.36_spmd, body=%wide.region_34.35_spmd.sunk | while | flops 765635584 | bytes 45661068 | solution.py:153
  901.6 6.4 copy.302
  908.1 6.4 copy.301
  923.0 60.5 %reduce-scatter.16.cloned.1.call-done = bf16[1024,128]{1,0:T(8,128)(2,1)} async-done(((bf16[16384,128]{1,0:T(8,128)(2,1)}), bf16[1024,128]{1,0:T(8,128)(2,1)}) %reduce-scatter.16.cloned.1.call-update) | async-done | bytes 262160 | tf_op jit(solution)/shard_map/reduce_scatter | solution.py:276
  983.5 81.2 %reduce-scatter.14.cloned.1.call-done = bf16[1024,128]{1,0:T(8,128)(2,1)} async-done(((bf16[16384,128]{1,0:T(8,128)(2,1)}), bf16[1024,128]{1,0:T(8,128)(2,1)}) %reduce-scatter.14.cloned.1.call-update) | async-done | bytes 262160 | tf_op jit(solution)/shard_map/reduce_scatter | solution.py:273
  1067.5 4.4 all-to-all-start.3
  1072.1 19.8 %all-to-all-done.3 = bf16[3,1024,128]{2,0,1:T(4,128)(2,1)S(1)} async-done(((bf16[3,1024,128]{2,0,1:T(4,128)(2,1)}), bf16[3,1024,128]{2,0,1:T(4,128)(2,1)S(1)}, u32[]{:S(2)}, u32[]{:S(2)}) %all-to-all-start.3) | async-done | bytes 786464 | tf_op jit(solution)/shard_map/all_to_all | solution.py:281
  1095.3 4.2 fusion.216
  1103.3 4.6 convolution_convert_fusion
  1108.0 64.7 %psum.46 = bf16[1024]{0:T(1024)(128)(2,1)S(1)} all-reduce(bf16[1024]{0:T(1024)(128)(2,1)S(1)} %get-tuple-element.1920), channel_id=1, replica_groups=mesh['seq'=8,'blk'=4,'tp'=4] {'seq','blk'}, use_global_device_ids=true, to_apply=%region_56.57 | all-reduce | flops 1024 | bytes 4096 | tf_op jit(solution)/shard_map/psum | solution.py:325
  1173.2 10.0 all-reduce.5.cloned.1.call-done
  1183.2 4.2 convert_element_type.415
  1190.9 72.7 %reduce-scatter.22.cloned.1.call-done = bf16[32,8]{1,0:T(8,128)(2,1)} async-done(((bf16[1024,8]{1,0:T(8,128)(2,1)}), bf16[32,8]{1,0:T(8,128)(2,1)}) %reduce-scatter.22.cloned.1.call-update) | async-done | bytes 528
  1264.4 10.4 psum.42
  1274.8 70.6 %reduce-scatter.20.cloned.1.call-done = bf16[32,1024]{1,0:T(8,128)(2,1)} async-done(((bf16[1024,1024]{1,0:T(8,128)(2,1)}), bf16[32,1024]{1,0:T(8,128)(2,1)}) %reduce-scatter.20.cloned.1.call-update) | async-done | bytes 65552 | tf_op jit(solution)/shard_map/reduce_scatter | solution.py:311
  1345.4 89.2 %reduce-scatter.18.cloned.1.call-done = bf16[32,3072]{1,0:T(8,128)(2,1)} async-done(((bf16[1024,3072]{1,0:T(8,128)(2,1)}), bf16[32,3072]{1,0:T(8,128)(2,1)}) %reduce-scatter.18.cloned.1.call-update) | async-done | bytes 196624 | tf_op jit(solution)/shard_map/reduce_scatter | solution.py:308
  1435.7 42.4 %all-reduce.7.cloned.1.call-done = (bf16[32,3072]{1,0:T(8,128)(2,1)}, bf16[32,1024]{1,0:T(8,128)(2,1)}) async-done(((bf16[32,3072]{1,0:T(8,128)(2,1)}, bf16[32,1024]{1,0:T(8,128)(2,1)}), (bf16[32,3072]{1,0:T(8,128)(2,1)}, bf16[32,1024]{1,0:T(8,128)(2,1)})) %all-reduce.7.cloned.1.call-update) | async-done | bytes 262160 | tf_op jit(solution)/shard_map/psum | solution.py:319
  (3241 shorter events, 650.2 us)
Async XLA Ops:
  7.2 435.6 %copy-start = (bf16[1024,1024]{1,0:T(8,128)(2,1)S(1)}, bf16[1024,1024]{1,0:T(8,128)(2,1)}, u32[]{:S(2)}) copy-start(bf16[1024,1024]{1,0:T(8,128)(2,1)} %param.101) | copy-start | bytes 6291460
  7.2 95.3 %all-gather.7.cloned.1.call-start = ((), (), s32[]{:S(2)}) async-start(), calls=%async_computation.12 | async-start | bytes 4456448 | tf_op jit(solution)/shard_map/all_gather | solution.py:166
  8.5 10.9 copy-start.16
  9.6 9.7 copy-start.18
  10.4 8.9 copy-start.2
  10.4 8.9 copy-start.11
  10.5 8.9 copy-start.13
  51.4 105.1 %all-gather.5.cloned.1.call-start = ((), (), s32[]{:S(2)}) async-start(), calls=%async_computation.11 | async-start | bytes 4456448 | tf_op jit(solution)/shard_map/all_gather | solution.py:165
  52.5 363.9 %all-gather.9.cloned.1.call-start = ((), (), s32[]{:S(2)}) async-start(), calls=%async_computation.13 | async-start | bytes 1310720 | tf_op jit(solution)/shard_map/all_gather | solution.py:179
  376.7 14.5 copy-start.20
  394.6 48.2 %all-gather.11.cloned.1.call-start = ((), (), s32[]{:S(2)}) async-start(), calls=%async_computation.15 | async-start | bytes 1310720 | tf_op jit(solution)/shard_map/all_gather | solution.py:191
  396.7 46.1 %copy-start.26 = (f32[1024]{0:T(1024)S(1)}, f32[1024]{0:T(1024)}, u32[]{:S(2)}) copy-start(f32[1024]{0:T(1024)} %param.100) | copy-start | bytes 12292
  396.7 77.8 %reduce-scatter.12.cloned.1.call-start = ((), (), s32[]{:S(2)}) async-start(), calls=%async_computation.16 | async-start | bytes 1310720 | tf_op jit(solution)/shard_map/reduce_scatter | solution.py:203
  442.8 5.4 copy-start.23
  450.5 50.2 %copy-start.22 = (f32[1024]{0:T(1024)S(1)}, f32[1024]{0:T(1024)}, u32[]{:S(2)}) copy-start(f32[1024]{0:T(1024)} %param.102) | copy-start | bytes 12292
  450.5 50.2 %reduce-scatter.10.cloned.1.call-start = ((), (), s32[]{:S(2)}) async-start(), calls=%async_computation.14 | async-start | bytes 1310720 | tf_op jit(solution)/shard_map/reduce_scatter | solution.py:183
  454.7 49.1 %copy-start.3 = (bf16[1024,1024]{1,0:T(8,128)(2,1)S(1)}, bf16[1024,1024]{1,0:T(8,128)(2,1)}, u32[]{:S(2)}) copy-start(bf16[1024,1024]{1,0:T(8,128)(2,1)} %param.95) | copy-start | bytes 6291460
  505.5 12.0 all-to-all-start.2
  509.9 8.3 copy-start.8
  509.9 473.6 %reduce-scatter.16.cloned.1.call-start = ((), (), s32[]{:S(2)}) async-start(), calls=%async_computation.18 | async-start | bytes 4456448 | tf_op jit(solution)/shard_map/reduce_scatter | solution.py:276
  908.0 156.7 %reduce-scatter.14.cloned.1.call-start = ((), (), s32[]{:S(2)}) async-start(), calls=%async_computation.17 | async-start | bytes 4456448 | tf_op jit(solution)/shard_map/reduce_scatter | solution.py:273
  914.5 268.7 %all-reduce.5.cloned.1.call-start = ((), (), s32[]{:S(2)}) async-start(), calls=%async_computation.22 | async-start | bytes 8388608 | tf_op jit(solution)/shard_map/psum | solution.py:324
  1065.8 6.1 copy-start.7
  1067.5 24.5 %all-to-all-start.3 = ((bf16[3,1024,128]{2,0,1:T(4,128)(2,1)}), bf16[3,1024,128]{2,0,1:T(4,128)(2,1)S(1)}, u32[]{:S(2)}, u32[]{:S(2)}) async-start(bf16[3,1024,128]{2,0,1:T(4,128)(2,1)} %copy.303), calls=%async_computation.7 | async-start | bytes 2097152 | tf_op jit(solution)/shard_map/all_to_all | solution.py:281
  1071.9 191.8 %reduce-scatter.22.cloned.1.call-start = ((), (), s32[]{:S(2)}) async-start(), calls=%async_computation.21 | async-start | bytes 270336
  1072.0 23.3 %copy-start.12 = (f32[1024]{0:T(1024)S(1)}, f32[1024]{0:T(1024)}, u32[]{:S(2)}) copy-start(f32[1024]{0:T(1024)} %param.91) | copy-start | bytes 12292
  1072.0 23.3 %copy-start.17 = (f32[128]{0:T(128)S(1)}, f32[128]{0:T(128)}, u32[]{:S(2)}) copy-start(f32[128]{0:T(128)} %copy-done.16) | copy-start | bytes 1540
  1072.0 23.3 %copy-start.19 = (f32[128]{0:T(128)S(1)}, f32[128]{0:T(128)}, u32[]{:S(2)}) copy-start(f32[128]{0:T(128)} %copy-done.18) | copy-start | bytes 1540
  1100.5 244.9 %reduce-scatter.20.cloned.1.call-start = ((), (), s32[]{:S(2)}) async-start(), calls=%async_computation.20 | async-start | bytes 2162688 | tf_op jit(solution)/shard_map/reduce_scatter | solution.py:311
  1102.6 331.9 %reduce-scatter.18.cloned.1.call-start = ((), (), s32[]{:S(2)}) async-start(), calls=%async_computation.19 | async-start | bytes 6488064 | tf_op jit(solution)/shard_map/reduce_scatter | solution.py:308
  1107.9 370.2 %all-reduce.7.cloned.1.call-start = ((), (), s32[]{:S(2)}) async-start(), calls=%async_computation.23 | async-start | bytes 524288 | tf_op jit(solution)/shard_map/psum | solution.py:319
  1187.4 293.9 %copy-start.1 = (bf16[1024,1024]{1,0:T(8,128)(2,1)S(1)}, bf16[1024,1024]{1,0:T(8,128)(2,1)}, u32[]{:S(2)}) copy-start(bf16[1024,1024]{1,0:T(8,128)(2,1)} %param.101) | copy-start | bytes 6291460
  (12 other events, 34.2 us)
Sparse Core Ops, SparseCore 0:
  51.5 50.9 all-gather.6
  105.2 51.1 all-gather.4
  394.7 21.6 all-gather.8
  418.5 24.2 all-gather.10
  450.7 23.8 reduce-scatter.11
  477.5 23.2 reduce-scatter.9
  908.1 75.2 reduce-scatter.15
  987.8 76.8 reduce-scatter.13
  1068.7 114.4 all-reduce.4
  1187.0 76.5 reduce-scatter.21
  1267.2 78.1 reduce-scatter.19
  1349.0 85.5 reduce-scatter.17
  1437.2 40.8 all-reduce.6
where the time goes:
time: 1500 us; the launch traced here: 1490 us
  waiting for transfers between devices  639 us (43%)
  matrix products  276 us (18%)
  local copies, waits for them, and re-layouts  249 us (17%)
  other arithmetic  174 us (12%)
  blocking collectives  108 us (7%)
  loops' own time  17.9 us (1%)
    reduce_scatter x1, waiting for transfers between devices, per_device(): lax.psum_scatter(qkv_weight_grad.astype(jnp.bfloat16), ('seq', 'blk'), sc...  89.2 us
    dot_general x256, matrix products, block_scores(): jnp.einsum('qhd,khd->hqk', split_heads(query_heads[low_row:]), split_head...  82.9 us
    reduce_scatter x1, waiting for transfers between devices, per_device(): lax.psum_scatter(key_grad.astype(jnp.bfloat16), ('blk', 'tp'), scatter_di...  81.2 us
    dynamic_update_slice x128, local copies, waits for them, and re-layouts, backward_update(): lax.dynamic_update_slice_in_dim(value_grad, value_part, first_key, 0)  79.2 us
    scatter x112, other arithmetic, forward_update(): run_sum.at[:, low_row:].set(new_sum)  75 us
    unnamed x14, waiting for transfers between devices  72.9 us
    reduce_scatter x1, waiting for transfers between devices, per_device(): lax.psum_scatter(out_weight_grad.astype(jnp.bfloat16), ('seq', 'blk'), sc...  70.6 us
    dynamic_update_slice x112, local copies, waits for them, and re-layouts, backward_update(): lax.dynamic_update_slice_in_dim(key_grad, key_part, first_key, 0)  69 us
  transfers between devices with their start and end apart: 15, of which 15 were waited for; matrix products, arithmetic and copies ran while one was open for 4% of the time, Pallas kernels for 0%

commit v1 on v0

--- a/solution.py
+++ b/solution.py
@@ -158,13 +158,19 @@
         jnp.zeros((query_rows, head_cols), jnp.float32),
     )
     cycle_init = (initial_state,)
+    note_words = lambda here_x, d0: jnp.concatenate(
+        lax.all_to_all(
+            jnp.stack([here_x for _ in range(lax.axis_size(("blk", "tp")))]),
+            split_axis=0,
+            concat_axis=0,
+            axis_name=("blk", "tp"),
+        ),
+        d0,
+    )
     run_max, run_sum, run_acc = fold_with(
         forward_update,
         cycle_init[0],
-        (
-            lax.all_gather(key_heads, ("blk", "tp"), axis=0, tiled=True),
-            lax.all_gather(value_heads, ("blk", "tp"), axis=0, tiled=True),
-        ),
+        (note_words(key_heads, 0), lax.all_gather(value_heads, ("blk", "tp"), axis=0, tiled=True)),
     )
     context_heads = (run_acc / jnp.repeat(run_sum.T, head_dim, axis=1)).astype(jnp.bfloat16)
     log_total = run_max + jnp.log(run_sum)

time: 1500 us -> 1940 us (1.29)
  local copies, waits for them, and re-layouts: 249 us -> 565 us
  matrix products: 276 us -> 360 us
    while x16 -> x784, local copies, waits for them, and re-layouts: 0.03 us -> 203 us
    dot_general x256, matrix products: 82.9 us -> 167 us  [block_scores(): jnp.einsum('qhd,khd->hqk', split_heads(query_heads[low_row:]), split_head...]
    slice x224, local copies, waits for them, and re-layouts: 3.17 us -> 76.2 us  [block_scores(): query_heads[low_row:]]
    all_to_all x0 -> x1, waiting for transfers between devices: none -> 66.5 us  [per_device(): lax.all_to_all(jnp.stack([here_x for _ in range(lax.axis_size(('blk', 'tp...]
    all_gather x1, waiting for transfers between devices: 45 us -> 5.51 us  [per_device(): lax.all_gather(value_heads, ('blk', 'tp'), axis=0, tiled=True)]
    slice x16 -> x32, local copies, waits for them, and re-layouts: 14.8 us -> 40.2 us  [by_segments(): key_shard[low_row:low_row + local_tokens]]
where the time goes in v1:
time: 1940 us; the launch traced here: 1920 us
  waiting for transfers between devices  648 us (33%)
  local copies, waits for them, and re-layouts  565 us (29%)
  matrix products  360 us (19%)
  other arithmetic  185 us (10%)
  blocking collectives  106 us (5%)
  loops' own time  20.4 us (1%)
    while x784, local copies, waits for them, and re-layouts  203 us
    dot_general x256, matrix products, block_scores(): jnp.einsum('qhd,khd->hqk', split_heads(query_heads[low_row:]), split_head...  167 us
    reduce_scatter x1, waiting for transfers between devices, per_device(): lax.psum_scatter(qkv_weight_grad.astype(jnp.bfloat16), ('seq', 'blk'), sc...  89.2 us
    reduce_scatter x1, waiting for transfers between devices, per_device(): lax.psum_scatter(key_grad.astype(jnp.bfloat16), ('blk', 'tp'), scatter_di...  81.2 us
    dynamic_update_slice x128, local copies, waits for them, and re-layouts, backward_update(): lax.dynamic_update_slice_in_dim(value_grad, value_part, first_key, 0)  79.2 us
    slice x224, local copies, waits for them, and re-layouts, block_scores(): query_heads[low_row:]  76.2 us
    scatter x112, other arithmetic, forward_update(): run_sum.at[:, low_row:].set(new_sum)  75.7 us
    unnamed x14, waiting for transfers between devices  73.4 us

profile of v1, /device:TPU:0, one launch (start us, length us, event | category | flops | bytes accessed | tf_op | source)
XLA Modules:
  0.0 1917.8 jit_solution(1806991275964906481)
XLA Ops:
  10.5 8.7 copy.287
  19.3 5.0 fusion.199
  25.8 21.5 %all_to_all.76 = bf16[3,128,1024]{1,0,2:T(4,128)(2,1)S(1)} all-to-all(bf16[3,128,1024]{1,0,2:T(4,128)(2,1)} %copy.289), channel_id=1, replica_groups=mesh['seq'=8,'blk'=4,'tp'=4] {'seq'}, dimensions={2} | all-to-all | bytes 1572864 | tf_op jit(solution)/shard_map/all_to_all | solution.py:73
  52.5 7.1 all-to-all-start.1
  64.9 66.5 %all-to-all-done.1 = bf16[16,1024,128]{1,2,0:T(8,128)(2,1)} async-done(((bf16[16,1024,128]{1,2,0:T(8,128)(2,1)}), bf16[16,1024,128]{1,2,0:T(8,128)(2,1)}, u32[]{:S(2)}, u32[]{:S(2)}) %all-to-all-start.1) | async-done | bytes 4194336 | tf_op jit(solution)/shard_map/all_to_all | solution.py:162
  131.4 6.4 copy.291
  137.8 5.5 all-gather.5.cloned.1.call-done
  144.0 626.6 %while.112 = (s32[]{:T(128)}, f32[2,1024]{1,0:T(2,128)S(1)}, f32[2,1024]{1,0:T(2,128)}, f32[1024,128]{0,1:T(8,128)S(1)}, s32[1024]{0:T(1024)S(1)}, /*index=5*/bf...) while((s32[]{:T(128)}, f32[2,1024]{1,0:T(2,128)S(1)}, ...), condition=%wide.region_26.27_spmd, body=%wide.region_9.26_spmd.sunk | while | flops 314464256 | bytes 39362704 | solution.py:153
  773.2 9.9 all_to_all.77
  790.1 18.1 all-gather.7.cloned.1.call-done
  808.2 4.5 fusion.274
  812.7 22.1 %all-gather.9.cloned.1.call-done = bf16[512,1024]{1,0:T(8,128)(2,1)} async-done(((bf16[128,1024]{1,0:T(8,128)(2,1)}), bf16[512,1024]{1,0:T(8,128)(2,1)}) %all-gather.9.cloned.1.call-update) | async-done | bytes 1048592 | tf_op jit(solution)/shard_map/all_gather | solution.py:197
  834.8 5.0 fusion.257
  847.8 19.3 %reduce-scatter.12.cloned.1.call-done = bf16[128,1024]{1,0:T(8,128)(2,1)} async-done(((bf16[512,1024]{1,0:T(8,128)(2,1)}), bf16[128,1024]{1,0:T(8,128)(2,1)}) %reduce-scatter.12.cloned.1.call-update) | async-done | bytes 262160 | tf_op jit(solution)/shard_map/reduce_scatter | solution.py:209
  868.9 24.4 %reduce-scatter.10.cloned.1.call-done = bf16[128,1024]{1,0:T(8,128)(2,1)} async-done(((bf16[512,1024]{1,0:T(8,128)(2,1)}), bf16[128,1024]{1,0:T(8,128)(2,1)}) %reduce-scatter.10.cloned.1.call-update) | async-done | bytes 262160 | tf_op jit(solution)/shard_map/reduce_scatter | solution.py:189
  903.2 7.3 all-to-all-done.3
  911.3 35.2 %all-gather.11.cloned.1.call-done = bf16[16384,128]{0,1:T(8,128)(2,1)} async-done(((bf16[1024,128]{0,1:T(8,128)(2,1)}), bf16[16384,128]{0,1:T(8,128)(2,1)}) %all-gather.11.cloned.1.call-update) | async-done | bytes 4194320 | tf_op jit(solution)/shard_map/all_gather | solution.py:274
  951.4 378.1 %while.113 = (s32[]{:T(128)}, f32[1024,128]{0,1:T(8,128)S(1)}, bf16[16384,128]{0,1:T(8,128)(2,1)}, bf16[16384,128]{0,1:T(8,128)(2,1)}, bf16[16384,128]{0,1:T(8,1...) while((s32[]{:T(128)}, f32[1024,128]{0,1:T(8,128)S(1)}, ...), condition=%wide.region_35.36_spmd, body=%wide.region_34.35_spmd.sunk | while | flops 765635584 | bytes 45661068 | solution.py:153
  1329.5 6.4 copy.304
  1336.0 6.4 copy.303
  1350.7 62.5 %reduce-scatter.16.cloned.1.call-done = bf16[1024,128]{1,0:T(8,128)(2,1)} async-done(((bf16[16384,128]{1,0:T(8,128)(2,1)}), bf16[1024,128]{1,0:T(8,128)(2,1)}) %reduce-scatter.16.cloned.1.call-update) | async-done | bytes 262160 | tf_op jit(solution)/shard_map/reduce_scatter | solution.py:282
  1413.2 81.2 %reduce-scatter.14.cloned.1.call-done = bf16[1024,128]{1,0:T(8,128)(2,1)} async-done(((bf16[16384,128]{1,0:T(8,128)(2,1)}), bf16[1024,128]{1,0:T(8,128)(2,1)}) %reduce-scatter.14.cloned.1.call-update) | async-done | bytes 262160 | tf_op jit(solution)/shard_map/reduce_scatter | solution.py:279
  1501.9 19.8 %all-to-all-done.4 = bf16[3,1024,128]{2,0,1:T(4,128)(2,1)S(1)} async-done(((bf16[3,1024,128]{2,0,1:T(4,128)(2,1)}), bf16[3,1024,128]{2,0,1:T(4,128)(2,1)S(1)}, u32[]{:S(2)}, u32[]{:S(2)}) %all-to-all-start.4) | async-done | bytes 786464 | tf_op jit(solution)/shard_map/all_to_all | solution.py:287
  1522.9 4.9 fusion.216
  1531.6 4.6 convolution_convert_fusion
  1536.9 64.4 %psum.46 = bf16[1024]{0:T(1024)(128)(2,1)S(1)} all-reduce(bf16[1024]{0:T(1024)(128)(2,1)S(1)} %copy-done.48), channel_id=1, replica_groups=mesh['seq'=8,'blk'=4,'tp'=4] {'seq','blk'}, use_global_device_ids=true, to_apply=%region_56.57 | all-reduce | flops 1024 | bytes 4096 | tf_op jit(solution)/shard_map/psum | solution.py:331
  1601.9 11.0 all-reduce.5.cloned.1.call-done
  1620.7 72.6 %reduce-scatter.22.cloned.1.call-done = bf16[32,8]{1,0:T(8,128)(2,1)} async-done(((bf16[1024,8]{1,0:T(8,128)(2,1)}), bf16[32,8]{1,0:T(8,128)(2,1)}) %reduce-scatter.22.cloned.1.call-update) | async-done | bytes 528
  1694.1 10.4 psum.42
  1704.6 70.6 %reduce-scatter.20.cloned.1.call-done = bf16[32,1024]{1,0:T(8,128)(2,1)} async-done(((bf16[1024,1024]{1,0:T(8,128)(2,1)}), bf16[32,1024]{1,0:T(8,128)(2,1)}) %reduce-scatter.20.cloned.1.call-update) | async-done | bytes 65552 | tf_op jit(solution)/shard_map/reduce_scatter | solution.py:317
  1775.1 89.2 %reduce-scatter.18.cloned.1.call-done = bf16[32,3072]{1,0:T(8,128)(2,1)} async-done(((bf16[1024,3072]{1,0:T(8,128)(2,1)}), bf16[32,3072]{1,0:T(8,128)(2,1)}) %reduce-scatter.18.cloned.1.call-update) | async-done | bytes 196624 | tf_op jit(solution)/shard_map/reduce_scatter | solution.py:314
  1865.4 42.4 %all-reduce.7.cloned.1.call-done = (bf16[32,3072]{1,0:T(8,128)(2,1)}, bf16[32,1024]{1,0:T(8,128)(2,1)}) async-done(((bf16[32,3072]{1,0:T(8,128)(2,1)}, bf16[32,1024]{1,0:T(8,128)(2,1)}), (bf16[32,3072]{1,0:T(8,128)(2,1)}, bf16[32,1024]{1,0:T(8,128)(2,1)})) %all-reduce.7.cloned.1.call-update) | async-done | bytes 262160 | tf_op jit(solution)/shard_map/psum | solution.py:325
  (4043 shorter events, 1069.6 us)
Async XLA Ops:
  7.2 827.6 %copy-start = (bf16[1024,1024]{1,0:T(8,128)(2,1)S(1)}, bf16[1024,1024]{1,0:T(8,128)(2,1)}, u32[]{:S(2)}) copy-start(bf16[1024,1024]{1,0:T(8,128)(2,1)} %param.101) | copy-start | bytes 6291460
  7.2 136.1 %all-gather.5.cloned.1.call-start = ((), (), s32[]{:S(2)}) async-start(), calls=%async_computation.12 | async-start | bytes 4456448 | tf_op jit(solution)/shard_map/all_gather | solution.py:173
  52.5 79.0 %all-to-all-start.1 = ((bf16[16,1024,128]{1,2,0:T(8,128)(2,1)}), bf16[16,1024,128]{1,2,0:T(8,128)(2,1)}, u32[]{:S(2)}, u32[]{:S(2)}) async-start(bf16[16,1024,128]{1,2,0:T(8,128)(2,1)} %stack.62), calls=%async_computation.1 | async-start | bytes 8388608 | tf_op jit(solution)/shard_map/all_to_all | solution.py:162
  59.6 748.6 %all-gather.7.cloned.1.call-start = ((), (), s32[]{:S(2)}) async-start(), calls=%async_computation.13 | async-start | bytes 1310720 | tf_op jit(solution)/shard_map/all_gather | solution.py:185
  146.5 20.0 %copy-start.11 = (bf16[256,128]{0,1:T(8,128)(2,1)S(1)}, bf16[256,128]{0,1:T(8,128)(2,1)}, u32[]{:S(2)}) copy-start(bf16[256,128]{0,1:T(8,128)(2,1)} %slice.2555) | copy-start | bytes 196612 | tf_op jit(solution)/shard_map/while
  185.7 20.0 %copy-start.11 = (bf16[256,128]{0,1:T(8,128)(2,1)S(1)}, bf16[256,128]{0,1:T(8,128)(2,1)}, u32[]{:S(2)}) copy-start(bf16[256,128]{0,1:T(8,128)(2,1)} %slice.2555) | copy-start | bytes 196612 | tf_op jit(solution)/shard_map/while
  224.8 20.0 %copy-start.11 = (bf16[256,128]{0,1:T(8,128)(2,1)S(1)}, bf16[256,128]{0,1:T(8,128)(2,1)}, u32[]{:S(2)}) copy-start(bf16[256,128]{0,1:T(8,128)(2,1)} %slice.2555) | copy-start | bytes 196612 | tf_op jit(solution)/shard_map/while
  303.1 20.0 %copy-start.11 = (bf16[256,128]{0,1:T(8,128)(2,1)S(1)}, bf16[256,128]{0,1:T(8,128)(2,1)}, u32[]{:S(2)}) copy-start(bf16[256,128]{0,1:T(8,128)(2,1)} %slice.2555) | copy-start | bytes 196612 | tf_op jit(solution)/shard_map/while
  342.3 20.0 %copy-start.11 = (bf16[256,128]{0,1:T(8,128)(2,1)S(1)}, bf16[256,128]{0,1:T(8,128)(2,1)}, u32[]{:S(2)}) copy-start(bf16[256,128]{0,1:T(8,128)(2,1)} %slice.2555) | copy-start | bytes 196612 | tf_op jit(solution)/shard_map/while
  459.8 20.0 %copy-start.11 = (bf16[256,128]{0,1:T(8,128)(2,1)S(1)}, bf16[256,128]{0,1:T(8,128)(2,1)}, u32[]{:S(2)}) copy-start(bf16[256,128]{0,1:T(8,128)(2,1)} %slice.2555) | copy-start | bytes 196612 | tf_op jit(solution)/shard_map/while
  498.9 20.0 %copy-start.11 = (bf16[256,128]{0,1:T(8,128)(2,1)S(1)}, bf16[256,128]{0,1:T(8,128)(2,1)}, u32[]{:S(2)}) copy-start(bf16[256,128]{0,1:T(8,128)(2,1)} %slice.2555) | copy-start | bytes 196612 | tf_op jit(solution)/shard_map/while
  616.4 20.0 %copy-start.11 = (bf16[256,128]{0,1:T(8,128)(2,1)S(1)}, bf16[256,128]{0,1:T(8,128)(2,1)}, u32[]{:S(2)}) copy-start(bf16[256,128]{0,1:T(8,128)(2,1)} %slice.2555) | copy-start | bytes 196612 | tf_op jit(solution)/shard_map/while
  787.3 47.4 %all-gather.9.cloned.1.call-start = ((), (), s32[]{:S(2)}) async-start(), calls=%async_computation.15 | async-start | bytes 1310720 | tf_op jit(solution)/shard_map/all_gather | solution.py:197
  789.5 45.3 %copy-start.52 = (f32[1024]{0:T(1024)S(1)}, f32[1024]{0:T(1024)}, u32[]{:S(2)}) copy-start(f32[1024]{0:T(1024)} %param.100) | copy-start | bytes 12292
  789.5 77.6 %reduce-scatter.12.cloned.1.call-start = ((), (), s32[]{:S(2)}) async-start(), calls=%async_computation.16 | async-start | bytes 1310720 | tf_op jit(solution)/shard_map/reduce_scatter | solution.py:209
  843.1 50.2 %reduce-scatter.10.cloned.1.call-start = ((), (), s32[]{:S(2)}) async-start(), calls=%async_computation.14 | async-start | bytes 1310720 | tf_op jit(solution)/shard_map/reduce_scatter | solution.py:189
  847.2 46.1 %copy-start.47 = (f32[1024]{0:T(1024)S(1)}, f32[1024]{0:T(1024)}, u32[]{:S(2)}) copy-start(f32[1024]{0:T(1024)} %param.102) | copy-start | bytes 12292
  847.2 49.6 %copy-start.8 = (bf16[1024,1024]{1,0:T(8,128)(2,1)S(1)}, bf16[1024,1024]{1,0:T(8,128)(2,1)}, u32[]{:S(2)}) copy-start(bf16[1024,1024]{1,0:T(8,128)(2,1)} %param.95) | copy-start | bytes 6291460
  847.2 99.3 %all-gather.11.cloned.1.call-start = ((), (), s32[]{:S(2)}) async-start(), calls=%async_computation.17 | async-start | bytes 4456448 | tf_op jit(solution)/shard_map/all_gather | solution.py:274
  898.5 12.0 all-to-all-start.3
  902.9 510.3 %reduce-scatter.16.cloned.1.call-start = ((), (), s32[]{:S(2)}) async-start(), calls=%async_computation.19 | async-start | bytes 4456448 | tf_op jit(solution)/shard_map/reduce_scatter | solution.py:282
  1335.9 158.5 %reduce-scatter.14.cloned.1.call-start = ((), (), s32[]{:S(2)}) async-start(), calls=%async_computation.18 | async-start | bytes 4456448 | tf_op jit(solution)/shard_map/reduce_scatter | solution.py:279
  1342.4 270.6 %all-reduce.5.cloned.1.call-start = ((), (), s32[]{:S(2)}) async-start(), calls=%async_computation.23 | async-start | bytes 8388608 | tf_op jit(solution)/shard_map/psum | solution.py:330
  1497.2 24.5 %all-to-all-start.4 = ((bf16[3,1024,128]{2,0,1:T(4,128)(2,1)}), bf16[3,1024,128]{2,0,1:T(4,128)(2,1)S(1)}, u32[]{:S(2)}, u32[]{:S(2)}) async-start(bf16[3,1024,128]{2,0,1:T(4,128)(2,1)} %copy.305), calls=%async_computation.8 | async-start | bytes 2097152 | tf_op jit(solution)/shard_map/all_to_all | solution.py:287
  1501.7 191.7 %reduce-scatter.22.cloned.1.call-start = ((), (), s32[]{:S(2)}) async-start(), calls=%async_computation.22 | async-start | bytes 270336
  1501.7 21.2 %copy-start.35 = (f32[1024]{0:T(1024)S(1)}, f32[1024]{0:T(1024)}, u32[]{:S(2)}) copy-start(f32[1024]{0:T(1024)} %param.91) | copy-start | bytes 12292
  1501.7 21.2 %copy-start.40 = (f32[128]{0:T(128)S(1)}, f32[128]{0:T(128)}, u32[]{:S(2)}) copy-start(f32[128]{0:T(128)} %copy-done.39) | copy-start | bytes 1540
  1501.7 21.2 %copy-start.42 = (f32[128]{0:T(128)S(1)}, f32[128]{0:T(128)}, u32[]{:S(2)}) copy-start(f32[128]{0:T(128)} %copy-done.41) | copy-start | bytes 1540
  1528.8 246.3 %reduce-scatter.20.cloned.1.call-start = ((), (), s32[]{:S(2)}) async-start(), calls=%async_computation.21 | async-start | bytes 2162688 | tf_op jit(solution)/shard_map/reduce_scatter | solution.py:317
  1531.0 333.4 %reduce-scatter.18.cloned.1.call-start = ((), (), s32[]{:S(2)}) async-start(), calls=%async_computation.20 | async-start | bytes 6488064 | tf_op jit(solution)/shard_map/reduce_scatter | solution.py:314
  1536.3 371.5 %all-reduce.7.cloned.1.call-start = ((), (), s32[]{:S(2)}) async-start(), calls=%async_computation.24 | async-start | bytes 524288 | tf_op jit(solution)/shard_map/psum | solution.py:325
  1617.2 293.9 %copy-start.1 = (bf16[1024,1024]{1,0:T(8,128)(2,1)S(1)}, bf16[1024,1024]{1,0:T(8,128)(2,1)}, u32[]{:S(2)}) copy-start(bf16[1024,1024]{1,0:T(8,128)(2,1)} %param.101) | copy-start | bytes 6291460
  (340 other events, 1474.0 us)
Sparse Core Ops, SparseCore 0:
  49.7 93.6 all-gather.4
  787.5 20.6 all-gather.6
  810.4 24.2 all-gather.8
  843.2 23.8 reduce-scatter.11
  870.0 23.1 reduce-scatter.9
  895.2 51.2 all-gather.10
  1336.0 77.1 reduce-scatter.15
  1417.5 76.8 reduce-scatter.13
  1498.4 114.4 all-reduce.4
  1616.8 76.5 reduce-scatter.21
  1696.9 78.1 reduce-scatter.19
  1778.7 85.5 reduce-scatter.17
  1866.9 40.8 all-reduce.6
